TPU v7x, 32 devices: a whole 2x2x4 slice. The times are simulated.
32 devices in a mesh: win: 8 (over z, y), seq: 4 (over x, core).
Axes of the slice: x: 2, y: 2, z: 4, core: 2. Of those that a mesh axis runs over, the one named last changes fastest.
Arguments:
- queries: bfloat16 [2, 8, 2048, 2048], P(None, 'win', 'seq'), may hold values from -4.5 to 4.5
- key_states: bfloat16 [2, 8, 2048, 2048], P(None, 'win', 'seq'), may hold values from -4.5 to 4.5
- value_states: bfloat16 [2, 8, 2048, 2048], P(None, 'win', 'seq'), may hold values from -5 to 5
- out_grad: bfloat16 [2, 8, 2048, 2048], P(None, 'win', 'seq'), may hold values from -60 to 60
Outputs:
- query_grad: bfloat16 [2, 8, 2048, 2048], P(None, 'win', 'seq')
- key_grad: bfloat16 [2, 8, 2048, 2048], P(None, 'win', 'seq')
- value_grad: bfloat16 [2, 8, 2048, 2048], P(None, 'win', 'seq')
All inputs are finite; a program needn't handle non-finite values.
Results may differ from a plain program's by a relative error of at most 0.0095.
Values may be sent and summed in bfloat16 or wider, within the bound.
No kernel may reach another device: no remote copies, remote signals or barrier semaphores. Data moves between devices by JAX's collectives and lax.ppermute only.
A program may use at most 192 MiB of HBM per device.

v0:
```python
import jax
import jax.numpy as jnp
from jax import lax
from jax.sharding import PartitionSpec as P

HEADS = 16
HDIM = 128
ROWS = 32
COLS = 64


def passed_along(block, axis, distance):
    devices = range(lax.axis_size(axis))
    route = [((i - distance) % len(devices), i) for i in devices]
    return lax.ppermute(block, axis, route)


def ahead_columns(values, col_axis):
    middle = values.shape[col_axis] // 2
    arrived = passed_along(lax.slice_in_dim(values, 0, middle, axis=col_axis), "win", -1)
    return jnp.concatenate(
        [lax.slice_in_dim(values, middle, 2 * middle, axis=col_axis), arrived], axis=col_axis
    )


def behind_columns(values, col_axis):
    middle = values.shape[col_axis] // 2
    arrived = passed_along(lax.slice_in_dim(values, middle, 2 * middle, axis=col_axis), "win", 1)
    return jnp.concatenate(
        [arrived, lax.slice_in_dim(values, 0, middle, axis=col_axis)], axis=col_axis
    )


def back_to_tokens(gradients):
    return lax.all_to_all(gradients, "seq", split_axis=2, concat_axis=3, tiled=True)


def window_grads(query_heads, key_heads, value_heads, grad_heads):
    samples_here, tokens, own_heads, head_size = query_heads.shape
    block_rows = min(512, tokens)
    factor = head_size ** (-0.5)

    def one_block(totals, offset):
        key_total, value_total = totals
        query_block = lax.dynamic_slice_in_dim(query_heads, offset, block_rows, 1)
        grad_block = lax.dynamic_slice_in_dim(grad_heads, offset, block_rows, 1)
        scores = (
            jnp.einsum(
                "bqhd,bkhd->bhqk", query_block, key_heads, preferred_element_type=jnp.float32
            )
            * factor
        )
        scores = scores - jnp.max(scores, axis=3, keepdims=True)
        weights = jnp.exp(scores)
        weights = weights / jnp.sum(weights, axis=3, keepdims=True)
        weights_low = weights.astype(jnp.bfloat16)
        value_total = value_total + jnp.einsum(
            "bhqk,bqhd->bkhd", weights_low, grad_block, preferred_element_type=jnp.float32
        )
        grad_probs = jnp.einsum(
            "bqhd,bkhd->bhqk", grad_block, value_heads, preferred_element_type=jnp.float32
        )
        row_dot = jnp.sum(weights * grad_probs, axis=3, keepdims=True)
        grad_scores = (weights * (grad_probs - row_dot) * factor).astype(jnp.bfloat16)
        query_block_grad = jnp.einsum(
            "bhqk,bkhd->bqhd", grad_scores, key_heads, preferred_element_type=jnp.float32
        ).astype(jnp.bfloat16)
        key_total = key_total + jnp.einsum(
            "bhqk,bqhd->bkhd", grad_scores, query_block, preferred_element_type=jnp.float32
        )
        return ((key_total, value_total), query_block_grad)

    starts = jnp.arange(tokens // block_rows, dtype=jnp.int32) * block_rows
    zero_acc = jnp.zeros(query_heads.shape, jnp.float32)
    (key_total, value_total), query_blocks = lax.scan(one_block, (zero_acc, zero_acc), starts)
    query_grad = jnp.moveaxis(query_blocks, 0, 1).reshape(
        samples_here, tokens, own_heads, head_size
    )
    return jnp.stack([query_grad, key_total.astype(jnp.bfloat16), value_total.astype(jnp.bfloat16)])


def on_device(queries, key_states, value_states, out_grad):
    samples = queries.shape[0]
    local_tokens = queries.shape[2]
    model_width = queries.shape[3]

    def head_view(values):
        return values.reshape(samples, local_tokens, HEADS, HDIM)

    sent_grad = head_view(out_grad)
    query_heads = lax.all_to_all(head_view(queries), "seq", split_axis=2, concat_axis=1, tiled=True)
    key_heads = lax.all_to_all(
        head_view(key_states), "seq", split_axis=2, concat_axis=1, tiled=True
    )
    value_heads = lax.all_to_all(
        head_view(value_states), "seq", split_axis=2, concat_axis=1, tiled=True
    )
    grad_heads = lax.all_to_all(sent_grad, "seq", split_axis=2, concat_axis=1, tiled=True)
    item_count, tokens, own_heads, head_size = query_heads.shape
    head_grid = grad_heads.reshape(item_count, ROWS, COLS, own_heads, head_size)
    head_grid = jnp.roll(ahead_columns(head_grid, 2), -(ROWS // 2), axis=1)
    grad_heads = head_grid.reshape(item_count, tokens, own_heads, head_size)
    gradients = window_grads(query_heads, key_heads, value_heads, grad_heads)
    back_grid = gradients.reshape(3, item_count, ROWS, COLS, own_heads, head_size)
    back_grid = behind_columns(jnp.roll(back_grid, ROWS // 2, axis=2), 3)
    gradients = back_grid.reshape(3, item_count, tokens, own_heads, head_size)
    result = gradients
    result = back_to_tokens(result)
    pieces = result.reshape(3, samples, 1, local_tokens, model_width)
    return (pieces[0], pieces[1], pieces[2])


def solution(mesh):
    placed = (
        P(None, "win", "seq", None),
        P(None, "win", "seq", None),
        P(None, "win", "seq", None),
        P(None, "win", "seq", None),
    )
    return jax.shard_map(
        on_device,
        mesh=mesh,
        in_specs=placed,
        out_specs=(
            P(None, "win", "seq", None),
            P(None, "win", "seq", None),
            P(None, "win", "seq", None),
        ),
        check_vma=False,
    )
```

profile of v0, /device:TPU:0, one launch (start us, length us, event | category | flops | bytes accessed | tf_op | source)
XLA Modules:
  0.0 1256.4 jit_solution(8506165742562413556)
XLA Ops:
  27.2 38.0 %all-to-all-done = bf16[2,512,16,128]{1,3,0,2:T(8,128)(2,1)} async-done(((bf16[2,512,16,128]{1,3,0,2:T(8,128)(2,1)}), bf16[2,512,16,128]{1,3,0,2:T(8,128)(2,1)}, u32[]{:S(2)}, u32[]{:S(2)}) %all-to-all-start) | async-done | bytes 4194336 | tf_op jit(solution)/shard_map/all_to_all | solution.py:91
  82.7 35.6 %all-to-all-done.1 = bf16[2,512,16,128]{1,3,0,2:T(8,128)(2,1)} async-done(((bf16[2,512,16,128]{1,3,0,2:T(8,128)(2,1)}), bf16[2,512,16,128]{1,3,0,2:T(8,128)(2,1)}, u32[]{:S(2)}, u32[]{:S(2)}) %all-to-all-start.1) | async-done | bytes 4194336 | tf_op jit(solution)/shard_map/all_to_all | solution.py:92
  133.9 37.4 %all-to-all-done.2 = bf16[2,512,16,128]{3,1,0,2:T(8,128)(2,1)} async-done(((bf16[2,512,16,128]{3,1,0,2:T(8,128)(2,1)}), bf16[2,512,16,128]{3,1,0,2:T(8,128)(2,1)}, u32[]{:S(2)}, u32[]{:S(2)}) %all-to-all-start.2) | async-done | bytes 4194336 | tf_op jit(solution)/shard_map/all_to_all | solution.py:98
  201.0 23.5 %all-to-all-done.3 = bf16[2,512,16,128]{1,3,0,2:T(8,128)(2,1)} async-done(((bf16[2,512,16,128]{1,3,0,2:T(8,128)(2,1)}), bf16[2,512,16,128]{1,3,0,2:T(8,128)(2,1)}, u32[]{:S(2)}, u32[]{:S(2)}) %all-to-all-start.3) | async-done | bytes 4194336 | tf_op jit(solution)/shard_map/all_to_all | solution.py:95
  224.4 7.3 copy.106
  237.0 600.8 %while.15 = (s32[]{:T(128)}, f32[2,2048,4,128]{1,3,2,0:T(8,128)}, f32[2,2048,4,128]{1,3,2,0:T(8,128)}, bf16[4,2,512,4,128]{4,2,0,3,1:T(8,128)(2,1)}, s32[4]{0:T(...) while((s32[]{:T(128)}, f32[2,2048,4,128]{1,3,2,0:T(8,128)}, ...), condition=%wide.region_4.5_spmd.clone, body=%wide.region_0.4_spmd.clone.sunk | while | flops 13069996032 | bytes 392267616 | solution.py:75
  239.6 18.1 %fusion.118 = f32[2,4,512,2048]{3,2,1,0:T(8,128)} fusion(bf16[2,2048,4,128]{3,1,2,0:T(8,128)(2,1)} %get-tuple-element.215, bf16[2,2048,4,128]{3,1,2,0:T(8,128)(2,1)} %get-tuple-element.214, s32[]{:T(128)S(6)} %select_n.6), kind=kOutput, calls=%fused_computation.21.clone.1 | convolution fusion | flops 2147483648 | bytes 38797316 | tf_op jit(solution)/shard_map/while/body/eval_jaxpr/bqhd,bkhd->bhqk/dot_general | solution.py:60
  257.7 17.5 %fusion.119 = (f32[2,4,512]{2,1,0:T(4,128)S(1)}, f32[2,4,512,2048]{3,2,1,0:T(8,128)}) fusion(bf16[2,2048,4,128]{3,1,2,0:T(8,128)(2,1)} %get-tuple-element.213, bf16[2,2048,4,128]{3,1,2,0:T(8,128)(2,1)} %get-tuple-element.212, s32[]{:T(128)S(6)} %select_n.6), kind=kOutput, calls=%fused_computation.49.clone.1 | convolution fusion | flops 2172651520 | bytes 38813700 | tf_op jit(solution)/shard_map/while/body/eval_jaxpr/sub | solution.py:53
  275.3 45.7 %fusion.120 = bf16[4,2,512,4,128]{4,2,0,3,1:T(8,128)(2,1)} fusion(bf16[4,2,512,4,128]{4,2,0,3,1:T(8,128)(2,1)} %get-tuple-element.198, s32[]{:T(128)S(6)} %copy.131, bf16[2,2048,4,128]{3,1,2,0:T(8,128)(2,1)} %get-tuple-element.213, f32[2,4,512,2048]{3,2,1,0:T(8,128)} %fusion.118, f32[2,4,512,2048]{3,2,1,0:T(8,128)} %get-tuple-element.181, ...), kind=kOutput, calls=%fused_computation.19.clone.1 | convolution fusion | flops 2206734336 | bytes 139493376 | tf_op jit(solution)/shard_map/while/body/eval_jaxpr/bhqk,bkhd->bqhd/dot_general | solution.py:65
  321.0 46.5 %bitcast_add_fusion.4 = f32[2,2048,4,128]{1,3,2,0:T(8,128)} fusion(f32[2,2048,4,128]{1,3,2,0:T(8,128)} %get-tuple-element.196, f32[2,4,512,2048]{3,2,1,0:T(8,128)} %fusion.118, pred[]{:T(512)S(6)} %compare.3, bf16[2,2048,4,128]{3,1,2,0:T(8,128)(2,1)} %get-tuple-element.212, s32[]{:T(128)S(6)} %select_n.6, ...), kind=kOutput, calls=%fused_computation.16.clone.1 | convolution fusion | flops 2210404352 | bytes 152076288 | tf_op jit(solution)/shard_map/while/body/eval_jaxpr/bhqk,bqhd->bkhd/dot_general | solution.py:68
  367.4 17.1 %bitcast_add_fusion.5 = f32[2,2048,4,128]{1,3,2,0:T(8,128)} fusion(f32[2,2048,4,128]{1,3,2,0:T(8,128)} %get-tuple-element.197, pred[]{:T(512)S(6)} %compare.3, bf16[2,2048,4,128]{3,1,2,0:T(8,128)(2,1)} %get-tuple-element.214, s32[]{:T(128)S(6)} %select_n.6, f32[2,4,512]{2,1,0:T(4,128)S(1)} %get-tuple-element.182, ...), kind=kOutput, calls=%fused_computation.15.clone.1 | convolution fusion | flops 4332722176 | bytes 23086592 | tf_op jit(solution)/shard_map/while/body/eval_jaxpr/bhqk,bqhd->bkhd/dot_general | solution.py:57
  387.1 18.1 %fusion.118 = f32[2,4,512,2048]{3,2,1,0:T(8,128)} fusion(bf16[2,2048,4,128]{3,1,2,0:T(8,128)(2,1)} %get-tuple-element.215, bf16[2,2048,4,128]{3,1,2,0:T(8,128)(2,1)} %get-tuple-element.214, s32[]{:T(128)S(6)} %select_n.6), kind=kOutput, calls=%fused_computation.21.clone.1 | convolution fusion | flops 2147483648 | bytes 38797316 | tf_op jit(solution)/shard_map/while/body/eval_jaxpr/bqhd,bkhd->bhqk/dot_general | solution.py:60
  405.2 17.5 %fusion.119 = (f32[2,4,512]{2,1,0:T(4,128)S(1)}, f32[2,4,512,2048]{3,2,1,0:T(8,128)}) fusion(bf16[2,2048,4,128]{3,1,2,0:T(8,128)(2,1)} %get-tuple-element.213, bf16[2,2048,4,128]{3,1,2,0:T(8,128)(2,1)} %get-tuple-element.212, s32[]{:T(128)S(6)} %select_n.6), kind=kOutput, calls=%fused_computation.49.clone.1 | convolution fusion | flops 2172651520 | bytes 38813700 | tf_op jit(solution)/shard_map/while/body/eval_jaxpr/sub | solution.py:53
  422.8 45.7 %fusion.120 = bf16[4,2,512,4,128]{4,2,0,3,1:T(8,128)(2,1)} fusion(bf16[4,2,512,4,128]{4,2,0,3,1:T(8,128)(2,1)} %get-tuple-element.198, s32[]{:T(128)S(6)} %copy.131, bf16[2,2048,4,128]{3,1,2,0:T(8,128)(2,1)} %get-tuple-element.213, f32[2,4,512,2048]{3,2,1,0:T(8,128)} %fusion.118, f32[2,4,512,2048]{3,2,1,0:T(8,128)} %get-tuple-element.181, ...), kind=kOutput, calls=%fused_computation.19.clone.1 | convolution fusion | flops 2206734336 | bytes 139493376 | tf_op jit(solution)/shard_map/while/body/eval_jaxpr/bhqk,bkhd->bqhd/dot_general | solution.py:65
  468.5 48.8 %bitcast_add_fusion.4 = f32[2,2048,4,128]{1,3,2,0:T(8,128)} fusion(f32[2,2048,4,128]{1,3,2,0:T(8,128)} %get-tuple-element.196, f32[2,4,512,2048]{3,2,1,0:T(8,128)} %fusion.118, pred[]{:T(512)S(6)} %compare.3, bf16[2,2048,4,128]{3,1,2,0:T(8,128)(2,1)} %get-tuple-element.212, s32[]{:T(128)S(6)} %select_n.6, ...), kind=kOutput, calls=%fused_computation.16.clone.1 | convolution fusion | flops 2210404352 | bytes 152076288 | tf_op jit(solution)/shard_map/while/body/eval_jaxpr/bhqk,bqhd->bkhd/dot_general | solution.py:68
  517.3 18.4 %bitcast_add_fusion.5 = f32[2,2048,4,128]{1,3,2,0:T(8,128)} fusion(f32[2,2048,4,128]{1,3,2,0:T(8,128)} %get-tuple-element.197, pred[]{:T(512)S(6)} %compare.3, bf16[2,2048,4,128]{3,1,2,0:T(8,128)(2,1)} %get-tuple-element.214, s32[]{:T(128)S(6)} %select_n.6, f32[2,4,512]{2,1,0:T(4,128)S(1)} %get-tuple-element.182, ...), kind=kOutput, calls=%fused_computation.15.clone.1 | convolution fusion | flops 4332722176 | bytes 23086592 | tf_op jit(solution)/shard_map/while/body/eval_jaxpr/bhqk,bqhd->bkhd/dot_general | solution.py:57
  538.2 18.1 %fusion.118 = f32[2,4,512,2048]{3,2,1,0:T(8,128)} fusion(bf16[2,2048,4,128]{3,1,2,0:T(8,128)(2,1)} %get-tuple-element.215, bf16[2,2048,4,128]{3,1,2,0:T(8,128)(2,1)} %get-tuple-element.214, s32[]{:T(128)S(6)} %select_n.6), kind=kOutput, calls=%fused_computation.21.clone.1 | convolution fusion | flops 2147483648 | bytes 38797316 | tf_op jit(solution)/shard_map/while/body/eval_jaxpr/bqhd,bkhd->bhqk/dot_general | solution.py:60
  556.4 17.5 %fusion.119 = (f32[2,4,512]{2,1,0:T(4,128)S(1)}, f32[2,4,512,2048]{3,2,1,0:T(8,128)}) fusion(bf16[2,2048,4,128]{3,1,2,0:T(8,128)(2,1)} %get-tuple-element.213, bf16[2,2048,4,128]{3,1,2,0:T(8,128)(2,1)} %get-tuple-element.212, s32[]{:T(128)S(6)} %select_n.6), kind=kOutput, calls=%fused_computation.49.clone.1 | convolution fusion | flops 2172651520 | bytes 38813700 | tf_op jit(solution)/shard_map/while/body/eval_jaxpr/sub | solution.py:53
  573.9 45.7 %fusion.120 = bf16[4,2,512,4,128]{4,2,0,3,1:T(8,128)(2,1)} fusion(bf16[4,2,512,4,128]{4,2,0,3,1:T(8,128)(2,1)} %get-tuple-element.198, s32[]{:T(128)S(6)} %copy.131, bf16[2,2048,4,128]{3,1,2,0:T(8,128)(2,1)} %get-tuple-element.213, f32[2,4,512,2048]{3,2,1,0:T(8,128)} %fusion.118, f32[2,4,512,2048]{3,2,1,0:T(8,128)} %get-tuple-element.181, ...), kind=kOutput, calls=%fused_computation.19.clone.1 | convolution fusion | flops 2206734336 | bytes 139493376 | tf_op jit(solution)/shard_map/while/body/eval_jaxpr/bhqk,bkhd->bqhd/dot_general | solution.py:65
  619.6 48.8 %bitcast_add_fusion.4 = f32[2,2048,4,128]{1,3,2,0:T(8,128)} fusion(f32[2,2048,4,128]{1,3,2,0:T(8,128)} %get-tuple-element.196, f32[2,4,512,2048]{3,2,1,0:T(8,128)} %fusion.118, pred[]{:T(512)S(6)} %compare.3, bf16[2,2048,4,128]{3,1,2,0:T(8,128)(2,1)} %get-tuple-element.212, s32[]{:T(128)S(6)} %select_n.6, ...), kind=kOutput, calls=%fused_computation.16.clone.1 | convolution fusion | flops 2210404352 | bytes 152076288 | tf_op jit(solution)/shard_map/while/body/eval_jaxpr/bhqk,bqhd->bkhd/dot_general | solution.py:68
  668.4 18.4 %bitcast_add_fusion.5 = f32[2,2048,4,128]{1,3,2,0:T(8,128)} fusion(f32[2,2048,4,128]{1,3,2,0:T(8,128)} %get-tuple-element.197, pred[]{:T(512)S(6)} %compare.3, bf16[2,2048,4,128]{3,1,2,0:T(8,128)(2,1)} %get-tuple-element.214, s32[]{:T(128)S(6)} %select_n.6, f32[2,4,512]{2,1,0:T(4,128)S(1)} %get-tuple-element.182, ...), kind=kOutput, calls=%fused_computation.15.clone.1 | convolution fusion | flops 4332722176 | bytes 23086592 | tf_op jit(solution)/shard_map/while/body/eval_jaxpr/bhqk,bqhd->bkhd/dot_general | solution.py:57
  689.3 18.1 %fusion.118 = f32[2,4,512,2048]{3,2,1,0:T(8,128)} fusion(bf16[2,2048,4,128]{3,1,2,0:T(8,128)(2,1)} %get-tuple-element.215, bf16[2,2048,4,128]{3,1,2,0:T(8,128)(2,1)} %get-tuple-element.214, s32[]{:T(128)S(6)} %select_n.6), kind=kOutput, calls=%fused_computation.21.clone.1 | convolution fusion | flops 2147483648 | bytes 38797316 | tf_op jit(solution)/shard_map/while/body/eval_jaxpr/bqhd,bkhd->bhqk/dot_general | solution.py:60
  707.5 17.5 %fusion.119 = (f32[2,4,512]{2,1,0:T(4,128)S(1)}, f32[2,4,512,2048]{3,2,1,0:T(8,128)}) fusion(bf16[2,2048,4,128]{3,1,2,0:T(8,128)(2,1)} %get-tuple-element.213, bf16[2,2048,4,128]{3,1,2,0:T(8,128)(2,1)} %get-tuple-element.212, s32[]{:T(128)S(6)} %select_n.6), kind=kOutput, calls=%fused_computation.49.clone.1 | convolution fusion | flops 2172651520 | bytes 38813700 | tf_op jit(solution)/shard_map/while/body/eval_jaxpr/sub | solution.py:53
  725.0 45.7 %fusion.120 = bf16[4,2,512,4,128]{4,2,0,3,1:T(8,128)(2,1)} fusion(bf16[4,2,512,4,128]{4,2,0,3,1:T(8,128)(2,1)} %get-tuple-element.198, s32[]{:T(128)S(6)} %copy.131, bf16[2,2048,4,128]{3,1,2,0:T(8,128)(2,1)} %get-tuple-element.213, f32[2,4,512,2048]{3,2,1,0:T(8,128)} %fusion.118, f32[2,4,512,2048]{3,2,1,0:T(8,128)} %get-tuple-element.181, ...), kind=kOutput, calls=%fused_computation.19.clone.1 | convolution fusion | flops 2206734336 | bytes 139493376 | tf_op jit(solution)/shard_map/while/body/eval_jaxpr/bhqk,bkhd->bqhd/dot_general | solution.py:65
  770.7 48.8 %bitcast_add_fusion.4 = f32[2,2048,4,128]{1,3,2,0:T(8,128)} fusion(f32[2,2048,4,128]{1,3,2,0:T(8,128)} %get-tuple-element.196, f32[2,4,512,2048]{3,2,1,0:T(8,128)} %fusion.118, pred[]{:T(512)S(6)} %compare.3, bf16[2,2048,4,128]{3,1,2,0:T(8,128)(2,1)} %get-tuple-element.212, s32[]{:T(128)S(6)} %select_n.6, ...), kind=kOutput, calls=%fused_computation.16.clone.1 | convolution fusion | flops 2210404352 | bytes 152076288 | tf_op jit(solution)/shard_map/while/body/eval_jaxpr/bhqk,bqhd->bkhd/dot_general | solution.py:68
  819.5 18.4 %bitcast_add_fusion.5 = f32[2,2048,4,128]{1,3,2,0:T(8,128)} fusion(f32[2,2048,4,128]{1,3,2,0:T(8,128)} %get-tuple-element.197, pred[]{:T(512)S(6)} %compare.3, bf16[2,2048,4,128]{3,1,2,0:T(8,128)(2,1)} %get-tuple-element.214, s32[]{:T(128)S(6)} %select_n.6, f32[2,4,512]{2,1,0:T(4,128)S(1)} %get-tuple-element.182, ...), kind=kOutput, calls=%fused_computation.15.clone.1 | convolution fusion | flops 4332722176 | bytes 23086592 | tf_op jit(solution)/shard_map/while/body/eval_jaxpr/bhqk,bqhd->bkhd/dot_general | solution.py:57
  865.0 138.7 %collective-permute-done.1 = bf16[3,2,32,32,4,128]{5,3,2,4,1,0:T(8,128)(2,1)S(1)} collective-permute-done((bf16[3,2,32,32,4,128]{5,3,2,4,1,0:T(8,128)(2,1)S(1)}, bf16[3,2,32,32,4,128]{5,3,2,4,1,0:T(8,128)(2,1)S(1)}, u32[]{:S(2)}, u32[]{:S(2)}) %collective-permute-start.1) | collective-permute-done | bytes 6291488 | tf_op jit(solution)/shard_map/ppermute | solution.py:15
  1005.3 50.2 %copy.110 = bf16[3,2,2048,4,128]{4,3,1,0,2:T(4,128)(2,1)S(1)} copy(bf16[3,2,2048,4,128]{4,2,3,1,0:T(8,128)(2,1)S(1)} %bitcast.70) | data formatting | bytes 25165824 | tf_op jit(solution)/shard_map/reshape | solution.py:106
  1055.6 141.0 %all_to_all.84 = bf16[3,2,2048,4,128]{4,3,1,0,2:T(4,128)(2,1)S(1)} all-to-all(bf16[3,2,2048,4,128]{4,3,1,0,2:T(4,128)(2,1)S(1)} %copy.110), channel_id=1, replica_groups=mesh['win'=8,'seq'=4] {'seq'}, dimensions={2} | all-to-all | bytes 25165824 | tf_op jit(solution)/shard_map/all_to_all | solution.py:35
  1196.5 14.8 %copy.111 = bf16[3,2,2048,4,128]{4,2,3,1,0:T(8,128)(2,1)S(1)} copy(bf16[3,2,2048,4,128]{4,3,1,0,2:T(4,128)(2,1)S(1)} %all_to_all.84) | data formatting | bytes 25165824 | tf_op jit(solution)/shard_map/all_to_all | solution.py:35
  1216.1 7.3 copy.114
  1229.6 7.3 copy.113
  (56 shorter events, 156.5 us)
Async XLA Ops:
  11.5 53.7 %all-to-all-start = ((bf16[2,512,16,128]{1,3,0,2:T(8,128)(2,1)}), bf16[2,512,16,128]{1,3,0,2:T(8,128)(2,1)}, u32[]{:S(2)}, u32[]{:S(2)}) async-start(bf16[2,512,16,128]{1,3,0,2:T(8,128)(2,1)} %copy.92), calls=%async_computation | async-start | bytes 8388608 | tf_op jit(solution)/shard_map/all_to_all | solution.py:91
  65.2 53.1 %all-to-all-start.1 = ((bf16[2,512,16,128]{1,3,0,2:T(8,128)(2,1)}), bf16[2,512,16,128]{1,3,0,2:T(8,128)(2,1)}, u32[]{:S(2)}, u32[]{:S(2)}) async-start(bf16[2,512,16,128]{1,3,0,2:T(8,128)(2,1)} %copy.96), calls=%async_computation.1 | async-start | bytes 8388608 | tf_op jit(solution)/shard_map/all_to_all | solution.py:92
  118.3 53.1 %all-to-all-start.2 = ((bf16[2,512,16,128]{3,1,0,2:T(8,128)(2,1)}), bf16[2,512,16,128]{3,1,0,2:T(8,128)(2,1)}, u32[]{:S(2)}, u32[]{:S(2)}) async-start(bf16[2,512,16,128]{3,1,0,2:T(8,128)(2,1)} %copy.100), calls=%async_computation.2 | async-start | bytes 8388608 | tf_op jit(solution)/shard_map/all_to_all | solution.py:98
  171.3 53.1 %all-to-all-start.3 = ((bf16[2,512,16,128]{1,3,0,2:T(8,128)(2,1)}), bf16[2,512,16,128]{1,3,0,2:T(8,128)(2,1)}, u32[]{:S(2)}, u32[]{:S(2)}) async-start(bf16[2,512,16,128]{1,3,0,2:T(8,128)(2,1)} %copy.104), calls=%async_computation.3 | async-start | bytes 8388608 | tf_op jit(solution)/shard_map/all_to_all | solution.py:95
  181.1 51.2 %collective-permute-start = (bf16[2,32,32,4,128]{4,2,1,3,0:T(8,128)(2,1)}, bf16[2,32,32,4,128]{4,2,1,3,0:T(8,128)(2,1)}, u32[]{:S(2)}, u32[]{:S(2)}) collective-permute-start(bf16[2,32,32,4,128]{4,2,1,3,0:T(8,128)(2,1)} %get-tuple-element.123), channel_id=1, source_target_pairs={{4,0},{8,4},{12,8},{16,12},{20,16},{24,20},{28,24},{0,28},{5,1},{9... | collective-permute-start | bytes 6291464 | tf_op jit(solution)/shard_map/ppermute | solution.py:15
  237.0 20.7 %copy-start = (s32[4]{0:T(128)}, s32[4]{0:T(128)S(1)}, u32[]{:S(2)}) copy-start(s32[4]{0:T(128)S(1)} %get-tuple-element.211) | copy-start | bytes 52 | tf_op jit(solution)/shard_map/while
  367.4 17.1 %copy-start.1 = (s32[4]{0:T(128)S(1)}, s32[4]{0:T(128)}, u32[]{:S(2)}) copy-start(s32[4]{0:T(128)} %copy-done) | copy-start | bytes 52 | tf_op jit(solution)/shard_map/while
  384.5 20.7 %copy-start = (s32[4]{0:T(128)}, s32[4]{0:T(128)S(1)}, u32[]{:S(2)}) copy-start(s32[4]{0:T(128)S(1)} %get-tuple-element.211) | copy-start | bytes 52 | tf_op jit(solution)/shard_map/while
  517.3 18.4 %copy-start.1 = (s32[4]{0:T(128)S(1)}, s32[4]{0:T(128)}, u32[]{:S(2)}) copy-start(s32[4]{0:T(128)} %copy-done) | copy-start | bytes 52 | tf_op jit(solution)/shard_map/while
  535.7 20.7 %copy-start = (s32[4]{0:T(128)}, s32[4]{0:T(128)S(1)}, u32[]{:S(2)}) copy-start(s32[4]{0:T(128)S(1)} %get-tuple-element.211) | copy-start | bytes 52 | tf_op jit(solution)/shard_map/while
  668.4 18.4 %copy-start.1 = (s32[4]{0:T(128)S(1)}, s32[4]{0:T(128)}, u32[]{:S(2)}) copy-start(s32[4]{0:T(128)} %copy-done) | copy-start | bytes 52 | tf_op jit(solution)/shard_map/while
  686.8 20.7 %copy-start = (s32[4]{0:T(128)}, s32[4]{0:T(128)S(1)}, u32[]{:S(2)}) copy-start(s32[4]{0:T(128)S(1)} %get-tuple-element.211) | copy-start | bytes 52 | tf_op jit(solution)/shard_map/while
  819.5 18.4 %copy-start.1 = (s32[4]{0:T(128)S(1)}, s32[4]{0:T(128)}, u32[]{:S(2)}) copy-start(s32[4]{0:T(128)} %copy-done) | copy-start | bytes 52 | tf_op jit(solution)/shard_map/while
  863.2 140.5 %collective-permute-start.1 = (bf16[3,2,32,32,4,128]{5,3,2,4,1,0:T(8,128)(2,1)S(1)}, bf16[3,2,32,32,4,128]{5,3,2,4,1,0:T(8,128)(2,1)S(1)}, u32[]{:S(2)}, u32[]{:S(2)}) collective-permute-start(bf16[3,2,32,32,4,128]{5,3,2,4,1,0:T(8,128)(2,1)S(1)} %fusion.72), channel_id=1, source_target_pairs={{28,0},{0,4},{4,8},{8,12},{12,16},{16,20},{20,24},{24,28},{29,1},{... | collective-permute-start | bytes 18874376 | tf_op jit(solution)/shard_map/ppermute | solution.py:15
where the time goes:
time: 1260 us
  matrix products  591 us (47%)
  waiting for transfers between devices  274 us (22%)
  local copies, waits for them, and re-layouts  203 us (16%)
  blocking collectives  141 us (11%)
  starting transfers between devices  26.6 us (2%)
  other arithmetic  13.4 us (1%)
    dot_general x4, matrix products, one_block(): jnp.einsum('bhqk,bqhd->bkhd', grad_scores, query_block, preferred_element...  193 us
    dot_general x4, matrix products, one_block(): jnp.einsum('bhqk,bkhd->bqhd', grad_scores, key_heads, preferred_element_t...  183 us
    all_to_all x1, blocking collectives, back_to_tokens(): lax.all_to_all(gradients, 'seq', split_axis=2, concat_axis=3, tiled=True)  141 us
    ppermute x2, waiting for transfers between devices, passed_along(): return lax.ppermute(block, axis, route)  139 us
    dot_general x4, matrix products, one_block(): jnp.einsum('bqhd,bkhd->bhqk', grad_block, value_heads, preferred_element_...  72.5 us
    dot_general x4, matrix products, one_block(): jnp.einsum('bhqk,bqhd->bkhd', weights_low, grad_block, preferred_element_...  72.2 us
    sub x4, matrix products, one_block(): scores = scores - jnp.max(scores, axis=3, keepdims=True)  70.1 us
    reshape x1, local copies, waits for them, and re-layouts, on_device(): gradients = back_grid.reshape(3, item_count, tokens, own_heads, head_size)  50.2 us
  transfers between devices with their start and end apart: 6, of which 6 were waited for; matrix products, arithmetic and copies ran while one was open for 5% of the time, Pallas kernels for 0%

commit v1 on v0

--- a/solution.py
+++ b/solution.py
@@ -32,7 +32,10 @@
 
 
 def back_to_tokens(gradients):
-    return lax.all_to_all(gradients, "seq", split_axis=2, concat_axis=3, tiled=True)
+    return jnp.concatenate(
+        lax.all_to_all(jnp.stack(jnp.split(gradients, lax.axis_size("seq"), axis=2)), "seq", 0, 0),
+        axis=3,
+    )
 
 
 def window_grads(query_heads, key_heads, value_heads, grad_heads):

time: 1260 us -> 1220 us (0.968)
  local copies, waits for them, and re-layouts: 203 us -> 141 us
  loops' own time: 7.64 us -> 22.1 us
    reshape x1 -> x0, local copies, waits for them, and re-layouts: 50.2 us -> none  [on_device(): gradients = back_grid.reshape(3, item_count, tokens, own_heads, head_size)]
    squeeze x0 -> x3, local copies, waits for them, and re-layouts: none -> 23.3 us  [on_device(): return (pieces[0], pieces[1], pieces[2])]
    unnamed x7 -> x4, local copies, waits for them, and re-layouts: 43.4 us -> 24.9 us
    all_to_all x1 -> x0, local copies, waits for them, and re-layouts: 14.8 us -> none  [back_to_tokens(): lax.all_to_all(gradients, 'seq', split_axis=2, concat_axis=3, tiled=True)]
    another operation x1, loops' own time: 7.64 us -> 22.1 us  [window_grads(): lax.scan(one_block, (zero_acc, zero_acc), starts)]
where the time goes in v1:
time: 1220 us; the launch traced here: 1210 us
  matrix products  591 us (48%)
  waiting for transfers between devices  274 us (22%)
  local copies, waits for them, and re-layouts  141 us (12%)
  blocking collectives  141 us (12%)
  starting transfers between devices  26.6 us (2%)
  loops' own time  22.1 us (2%)
  other arithmetic  15.1 us (1%)
    dot_general x4, matrix products, one_block(): jnp.einsum('bhqk,bqhd->bkhd', grad_scores, query_block, preferred_element...  193 us
    dot_general x4, matrix products, one_block(): jnp.einsum('bhqk,bkhd->bqhd', grad_scores, key_heads, preferred_element_t...  183 us
    all_to_all x1, blocking collectives, back_to_tokens(): lax.all_to_all(jnp.stack(jnp.split(gradients, lax.axis_size('seq'), axis=...  141 us
    ppermute x2, waiting for transfers between devices, passed_along(): return lax.ppermute(block, axis, route)  139 us
    dot_general x4, matrix products, one_block(): jnp.einsum('bqhd,bkhd->bhqk', grad_block, value_heads, preferred_element_...  72.5 us
    dot_general x4, matrix products, one_block(): jnp.einsum('bhqk,bqhd->bkhd', weights_low, grad_block, preferred_element_...  72.1 us
    sub x4, matrix products, one_block(): scores = scores - jnp.max(scores, axis=3, keepdims=True)  70.2 us
    all_to_all x1, waiting for transfers between devices, on_device(): lax.all_to_all(head_view(queries), 'seq', split_axis=2, concat_axis=1, ti...  38 us
  transfers between devices with their start and end apart: 6, of which 6 were waited for; matrix products, arithmetic and copies ran while one was open for 5% of the time, Pallas kernels for 0%

profile of v1, /device:TPU:0, one launch (start us, length us, event | category | flops | bytes accessed | tf_op | source)
XLA Modules:
  0.0 1211.2 jit_solution(15570510702407797911)
XLA Ops:
  27.2 38.0 %all-to-all-done = bf16[2,512,16,128]{1,3,0,2:T(8,128)(2,1)} async-done(((bf16[2,512,16,128]{1,3,0,2:T(8,128)(2,1)}), bf16[2,512,16,128]{1,3,0,2:T(8,128)(2,1)}, u32[]{:S(2)}, u32[]{:S(2)}) %all-to-all-start) | async-done | bytes 4194336 | tf_op jit(solution)/shard_map/all_to_all | solution.py:94
  82.7 35.6 %all-to-all-done.1 = bf16[2,512,16,128]{1,3,0,2:T(8,128)(2,1)} async-done(((bf16[2,512,16,128]{1,3,0,2:T(8,128)(2,1)}), bf16[2,512,16,128]{1,3,0,2:T(8,128)(2,1)}, u32[]{:S(2)}, u32[]{:S(2)}) %all-to-all-start.1) | async-done | bytes 4194336 | tf_op jit(solution)/shard_map/all_to_all | solution.py:95
  133.9 37.4 %all-to-all-done.2 = bf16[2,512,16,128]{3,1,0,2:T(8,128)(2,1)} async-done(((bf16[2,512,16,128]{3,1,0,2:T(8,128)(2,1)}), bf16[2,512,16,128]{3,1,0,2:T(8,128)(2,1)}, u32[]{:S(2)}, u32[]{:S(2)}) %all-to-all-start.2) | async-done | bytes 4194336 | tf_op jit(solution)/shard_map/all_to_all | solution.py:101
  201.0 23.5 %all-to-all-done.3 = bf16[2,512,16,128]{1,3,0,2:T(8,128)(2,1)} async-done(((bf16[2,512,16,128]{1,3,0,2:T(8,128)(2,1)}), bf16[2,512,16,128]{1,3,0,2:T(8,128)(2,1)}, u32[]{:S(2)}, u32[]{:S(2)}) %all-to-all-start.3) | async-done | bytes 4194336 | tf_op jit(solution)/shard_map/all_to_all | solution.py:98
  237.0 615.2 %while.15 = (s32[]{:T(128)}, f32[2,2048,4,128]{1,3,2,0:T(8,128)}, f32[2,2048,4,128]{1,3,2,0:T(8,128)}, bf16[4,2,512,4,128]{4,2,0,3,1:T(8,128)(2,1)}, s32[4]{0:T(...) while((s32[]{:T(128)}, f32[2,2048,4,128]{1,3,2,0:T(8,128)}, ...), condition=%wide.region_4.5_spmd.clone, body=%wide.region_0.4_spmd.clone.sunk | while | flops 13069996032 | bytes 392267616 | solution.py:78
  253.8 18.1 %fusion.118 = f32[2,4,512,2048]{3,2,1,0:T(8,128)} fusion(bf16[2,2048,4,128]{3,1,2,0:T(8,128)(2,1)} %get-tuple-element.207, bf16[2,2048,4,128]{3,1,2,0:T(8,128)(2,1)} %get-tuple-element.206, s32[]{:T(128)S(6)} %select_n.6), kind=kOutput, calls=%fused_computation.21.clone.1 | convolution fusion | flops 2147483648 | bytes 38797316 | tf_op jit(solution)/shard_map/while/body/eval_jaxpr/bqhd,bkhd->bhqk/dot_general | solution.py:63
  272.0 17.5 %fusion.119 = (f32[2,4,512]{2,1,0:T(4,128)S(1)}, f32[2,4,512,2048]{3,2,1,0:T(8,128)}) fusion(bf16[2,2048,4,128]{3,1,2,0:T(8,128)(2,1)} %get-tuple-element.205, bf16[2,2048,4,128]{3,1,2,0:T(8,128)(2,1)} %get-tuple-element.204, s32[]{:T(128)S(6)} %select_n.6), kind=kOutput, calls=%fused_computation.54.clone.1 | convolution fusion | flops 2172651520 | bytes 38813700 | tf_op jit(solution)/shard_map/while/body/eval_jaxpr/sub | solution.py:56
  289.5 45.7 %fusion.120 = bf16[4,2,512,4,128]{4,2,0,3,1:T(8,128)(2,1)} fusion(bf16[4,2,512,4,128]{4,2,0,3,1:T(8,128)(2,1)} %get-tuple-element.190, s32[]{:T(128)S(6)} %copy.120, bf16[2,2048,4,128]{3,1,2,0:T(8,128)(2,1)} %get-tuple-element.205, f32[2,4,512,2048]{3,2,1,0:T(8,128)} %fusion.118, f32[2,4,512,2048]{3,2,1,0:T(8,128)} %get-tuple-element.173, ...), kind=kOutput, calls=%fused_computation.19.clone.1 | convolution fusion | flops 2206734336 | bytes 139493376 | tf_op jit(solution)/shard_map/while/body/eval_jaxpr/bhqk,bkhd->bqhd/dot_general | solution.py:68
  335.2 46.5 %bitcast_add_fusion.4 = f32[2,2048,4,128]{1,3,2,0:T(8,128)} fusion(f32[2,2048,4,128]{1,3,2,0:T(8,128)} %get-tuple-element.188, f32[2,4,512,2048]{3,2,1,0:T(8,128)} %fusion.118, pred[]{:T(512)S(6)} %compare.3, bf16[2,2048,4,128]{3,1,2,0:T(8,128)(2,1)} %get-tuple-element.204, s32[]{:T(128)S(6)} %select_n.6, ...), kind=kOutput, calls=%fused_computation.16.clone.1 | convolution fusion | flops 2210404352 | bytes 152076288 | tf_op jit(solution)/shard_map/while/body/eval_jaxpr/bhqk,bqhd->bkhd/dot_general | solution.py:71
  381.7 17.1 %bitcast_add_fusion.5 = f32[2,2048,4,128]{1,3,2,0:T(8,128)} fusion(f32[2,2048,4,128]{1,3,2,0:T(8,128)} %get-tuple-element.189, pred[]{:T(512)S(6)} %compare.3, bf16[2,2048,4,128]{3,1,2,0:T(8,128)(2,1)} %get-tuple-element.206, s32[]{:T(128)S(6)} %select_n.6, f32[2,4,512]{2,1,0:T(4,128)S(1)} %get-tuple-element.174, ...), kind=kOutput, calls=%fused_computation.15.clone.1 | convolution fusion | flops 4332722176 | bytes 23086592 | tf_op jit(solution)/shard_map/while/body/eval_jaxpr/bhqk,bqhd->bkhd/dot_general | solution.py:60
  401.2 18.1 %fusion.118 = f32[2,4,512,2048]{3,2,1,0:T(8,128)} fusion(bf16[2,2048,4,128]{3,1,2,0:T(8,128)(2,1)} %get-tuple-element.207, bf16[2,2048,4,128]{3,1,2,0:T(8,128)(2,1)} %get-tuple-element.206, s32[]{:T(128)S(6)} %select_n.6), kind=kOutput, calls=%fused_computation.21.clone.1 | convolution fusion | flops 2147483648 | bytes 38797316 | tf_op jit(solution)/shard_map/while/body/eval_jaxpr/bqhd,bkhd->bhqk/dot_general | solution.py:63
  419.4 17.6 %fusion.119 = (f32[2,4,512]{2,1,0:T(4,128)S(1)}, f32[2,4,512,2048]{3,2,1,0:T(8,128)}) fusion(bf16[2,2048,4,128]{3,1,2,0:T(8,128)(2,1)} %get-tuple-element.205, bf16[2,2048,4,128]{3,1,2,0:T(8,128)(2,1)} %get-tuple-element.204, s32[]{:T(128)S(6)} %select_n.6), kind=kOutput, calls=%fused_computation.54.clone.1 | convolution fusion | flops 2172651520 | bytes 38813700 | tf_op jit(solution)/shard_map/while/body/eval_jaxpr/sub | solution.py:56
  436.9 45.7 %fusion.120 = bf16[4,2,512,4,128]{4,2,0,3,1:T(8,128)(2,1)} fusion(bf16[4,2,512,4,128]{4,2,0,3,1:T(8,128)(2,1)} %get-tuple-element.190, s32[]{:T(128)S(6)} %copy.120, bf16[2,2048,4,128]{3,1,2,0:T(8,128)(2,1)} %get-tuple-element.205, f32[2,4,512,2048]{3,2,1,0:T(8,128)} %fusion.118, f32[2,4,512,2048]{3,2,1,0:T(8,128)} %get-tuple-element.173, ...), kind=kOutput, calls=%fused_computation.19.clone.1 | convolution fusion | flops 2206734336 | bytes 139493376 | tf_op jit(solution)/shard_map/while/body/eval_jaxpr/bhqk,bkhd->bqhd/dot_general | solution.py:68
  482.6 48.8 %bitcast_add_fusion.4 = f32[2,2048,4,128]{1,3,2,0:T(8,128)} fusion(f32[2,2048,4,128]{1,3,2,0:T(8,128)} %get-tuple-element.188, f32[2,4,512,2048]{3,2,1,0:T(8,128)} %fusion.118, pred[]{:T(512)S(6)} %compare.3, bf16[2,2048,4,128]{3,1,2,0:T(8,128)(2,1)} %get-tuple-element.204, s32[]{:T(128)S(6)} %select_n.6, ...), kind=kOutput, calls=%fused_computation.16.clone.1 | convolution fusion | flops 2210404352 | bytes 152076288 | tf_op jit(solution)/shard_map/while/body/eval_jaxpr/bhqk,bqhd->bkhd/dot_general | solution.py:71
  531.5 18.3 %bitcast_add_fusion.5 = f32[2,2048,4,128]{1,3,2,0:T(8,128)} fusion(f32[2,2048,4,128]{1,3,2,0:T(8,128)} %get-tuple-element.189, pred[]{:T(512)S(6)} %compare.3, bf16[2,2048,4,128]{3,1,2,0:T(8,128)(2,1)} %get-tuple-element.206, s32[]{:T(128)S(6)} %select_n.6, f32[2,4,512]{2,1,0:T(4,128)S(1)} %get-tuple-element.174, ...), kind=kOutput, calls=%fused_computation.15.clone.1 | convolution fusion | flops 4332722176 | bytes 23086592 | tf_op jit(solution)/shard_map/while/body/eval_jaxpr/bhqk,bqhd->bkhd/dot_general | solution.py:60
  552.3 18.1 %fusion.118 = f32[2,4,512,2048]{3,2,1,0:T(8,128)} fusion(bf16[2,2048,4,128]{3,1,2,0:T(8,128)(2,1)} %get-tuple-element.207, bf16[2,2048,4,128]{3,1,2,0:T(8,128)(2,1)} %get-tuple-element.206, s32[]{:T(128)S(6)} %select_n.6), kind=kOutput, calls=%fused_computation.21.clone.1 | convolution fusion | flops 2147483648 | bytes 38797316 | tf_op jit(solution)/shard_map/while/body/eval_jaxpr/bqhd,bkhd->bhqk/dot_general | solution.py:63
  570.4 17.6 %fusion.119 = (f32[2,4,512]{2,1,0:T(4,128)S(1)}, f32[2,4,512,2048]{3,2,1,0:T(8,128)}) fusion(bf16[2,2048,4,128]{3,1,2,0:T(8,128)(2,1)} %get-tuple-element.205, bf16[2,2048,4,128]{3,1,2,0:T(8,128)(2,1)} %get-tuple-element.204, s32[]{:T(128)S(6)} %select_n.6), kind=kOutput, calls=%fused_computation.54.clone.1 | convolution fusion | flops 2172651520 | bytes 38813700 | tf_op jit(solution)/shard_map/while/body/eval_jaxpr/sub | solution.py:56
  587.9 45.7 %fusion.120 = bf16[4,2,512,4,128]{4,2,0,3,1:T(8,128)(2,1)} fusion(bf16[4,2,512,4,128]{4,2,0,3,1:T(8,128)(2,1)} %get-tuple-element.190, s32[]{:T(128)S(6)} %copy.120, bf16[2,2048,4,128]{3,1,2,0:T(8,128)(2,1)} %get-tuple-element.205, f32[2,4,512,2048]{3,2,1,0:T(8,128)} %fusion.118, f32[2,4,512,2048]{3,2,1,0:T(8,128)} %get-tuple-element.173, ...), kind=kOutput, calls=%fused_computation.19.clone.1 | convolution fusion | flops 2206734336 | bytes 139493376 | tf_op jit(solution)/shard_map/while/body/eval_jaxpr/bhqk,bkhd->bqhd/dot_general | solution.py:68
  633.7 48.8 %bitcast_add_fusion.4 = f32[2,2048,4,128]{1,3,2,0:T(8,128)} fusion(f32[2,2048,4,128]{1,3,2,0:T(8,128)} %get-tuple-element.188, f32[2,4,512,2048]{3,2,1,0:T(8,128)} %fusion.118, pred[]{:T(512)S(6)} %compare.3, bf16[2,2048,4,128]{3,1,2,0:T(8,128)(2,1)} %get-tuple-element.204, s32[]{:T(128)S(6)} %select_n.6, ...), kind=kOutput, calls=%fused_computation.16.clone.1 | convolution fusion | flops 2210404352 | bytes 152076288 | tf_op jit(solution)/shard_map/while/body/eval_jaxpr/bhqk,bqhd->bkhd/dot_general | solution.py:71
  682.5 18.3 %bitcast_add_fusion.5 = f32[2,2048,4,128]{1,3,2,0:T(8,128)} fusion(f32[2,2048,4,128]{1,3,2,0:T(8,128)} %get-tuple-element.189, pred[]{:T(512)S(6)} %compare.3, bf16[2,2048,4,128]{3,1,2,0:T(8,128)(2,1)} %get-tuple-element.206, s32[]{:T(128)S(6)} %select_n.6, f32[2,4,512]{2,1,0:T(4,128)S(1)} %get-tuple-element.174, ...), kind=kOutput, calls=%fused_computation.15.clone.1 | convolution fusion | flops 4332722176 | bytes 23086592 | tf_op jit(solution)/shard_map/while/body/eval_jaxpr/bhqk,bqhd->bkhd/dot_general | solution.py:60
  703.3 18.1 %fusion.118 = f32[2,4,512,2048]{3,2,1,0:T(8,128)} fusion(bf16[2,2048,4,128]{3,1,2,0:T(8,128)(2,1)} %get-tuple-element.207, bf16[2,2048,4,128]{3,1,2,0:T(8,128)(2,1)} %get-tuple-element.206, s32[]{:T(128)S(6)} %select_n.6), kind=kOutput, calls=%fused_computation.21.clone.1 | convolution fusion | flops 2147483648 | bytes 38797316 | tf_op jit(solution)/shard_map/while/body/eval_jaxpr/bqhd,bkhd->bhqk/dot_general | solution.py:63
  721.4 17.5 %fusion.119 = (f32[2,4,512]{2,1,0:T(4,128)S(1)}, f32[2,4,512,2048]{3,2,1,0:T(8,128)}) fusion(bf16[2,2048,4,128]{3,1,2,0:T(8,128)(2,1)} %get-tuple-element.205, bf16[2,2048,4,128]{3,1,2,0:T(8,128)(2,1)} %get-tuple-element.204, s32[]{:T(128)S(6)} %select_n.6), kind=kOutput, calls=%fused_computation.54.clone.1 | convolution fusion | flops 2172651520 | bytes 38813700 | tf_op jit(solution)/shard_map/while/body/eval_jaxpr/sub | solution.py:56
  739.0 45.7 %fusion.120 = bf16[4,2,512,4,128]{4,2,0,3,1:T(8,128)(2,1)} fusion(bf16[4,2,512,4,128]{4,2,0,3,1:T(8,128)(2,1)} %get-tuple-element.190, s32[]{:T(128)S(6)} %copy.120, bf16[2,2048,4,128]{3,1,2,0:T(8,128)(2,1)} %get-tuple-element.205, f32[2,4,512,2048]{3,2,1,0:T(8,128)} %fusion.118, f32[2,4,512,2048]{3,2,1,0:T(8,128)} %get-tuple-element.173, ...), kind=kOutput, calls=%fused_computation.19.clone.1 | convolution fusion | flops 2206734336 | bytes 139493376 | tf_op jit(solution)/shard_map/while/body/eval_jaxpr/bhqk,bkhd->bqhd/dot_general | solution.py:68
  784.7 48.8 %bitcast_add_fusion.4 = f32[2,2048,4,128]{1,3,2,0:T(8,128)} fusion(f32[2,2048,4,128]{1,3,2,0:T(8,128)} %get-tuple-element.188, f32[2,4,512,2048]{3,2,1,0:T(8,128)} %fusion.118, pred[]{:T(512)S(6)} %compare.3, bf16[2,2048,4,128]{3,1,2,0:T(8,128)(2,1)} %get-tuple-element.204, s32[]{:T(128)S(6)} %select_n.6, ...), kind=kOutput, calls=%fused_computation.16.clone.1 | convolution fusion | flops 2210404352 | bytes 152076288 | tf_op jit(solution)/shard_map/while/body/eval_jaxpr/bhqk,bqhd->bkhd/dot_general | solution.py:71
  833.5 18.3 %bitcast_add_fusion.5 = f32[2,2048,4,128]{1,3,2,0:T(8,128)} fusion(f32[2,2048,4,128]{1,3,2,0:T(8,128)} %get-tuple-element.189, pred[]{:T(512)S(6)} %compare.3, bf16[2,2048,4,128]{3,1,2,0:T(8,128)(2,1)} %get-tuple-element.206, s32[]{:T(128)S(6)} %select_n.6, f32[2,4,512]{2,1,0:T(4,128)S(1)} %get-tuple-element.174, ...), kind=kOutput, calls=%fused_computation.15.clone.1 | convolution fusion | flops 4332722176 | bytes 23086592 | tf_op jit(solution)/shard_map/while/body/eval_jaxpr/bhqk,bqhd->bkhd/dot_general | solution.py:60
  879.4 138.7 %collective-permute-done.1 = bf16[3,2,32,32,4,128]{5,3,2,4,1,0:T(8,128)(2,1)S(1)} collective-permute-done((bf16[3,2,32,32,4,128]{5,3,2,4,1,0:T(8,128)(2,1)S(1)}, bf16[3,2,32,32,4,128]{5,3,2,4,1,0:T(8,128)(2,1)S(1)}, u32[]{:S(2)}, u32[]{:S(2)}) %collective-permute-start.1) | collective-permute-done | bytes 6291488 | tf_op jit(solution)/shard_map/ppermute | solution.py:15
  1022.6 141.1 %all_to_all.74 = bf16[4,3,2,512,4,128]{5,3,4,2,1,0:T(8,128)(2,1)S(1)} all-to-all(bf16[4,3,2,512,4,128]{5,3,4,2,1,0:T(8,128)(2,1)S(1)} %pad_maximum_fusion.2), channel_id=1, replica_groups=mesh['win'=8,'seq'=4] {'seq'}, dimensions={0} | all-to-all | bytes 25165824 | tf_op jit(solution)/shard_map/all_to_all | solution.py:36
  1173.0 7.8 squeeze.15
  1180.8 7.4 copy.105
  1188.1 7.8 squeeze.14
  1195.9 7.4 copy.104
  1203.3 7.8 squeeze.13
  (56 shorter events, 145.2 us)
Async XLA Ops:
  11.5 53.7 %all-to-all-start = ((bf16[2,512,16,128]{1,3,0,2:T(8,128)(2,1)}), bf16[2,512,16,128]{1,3,0,2:T(8,128)(2,1)}, u32[]{:S(2)}, u32[]{:S(2)}) async-start(bf16[2,512,16,128]{1,3,0,2:T(8,128)(2,1)} %copy.86), calls=%async_computation | async-start | bytes 8388608 | tf_op jit(solution)/shard_map/all_to_all | solution.py:94
  65.2 53.0 %all-to-all-start.1 = ((bf16[2,512,16,128]{1,3,0,2:T(8,128)(2,1)}), bf16[2,512,16,128]{1,3,0,2:T(8,128)(2,1)}, u32[]{:S(2)}, u32[]{:S(2)}) async-start(bf16[2,512,16,128]{1,3,0,2:T(8,128)(2,1)} %copy.90), calls=%async_computation.1 | async-start | bytes 8388608 | tf_op jit(solution)/shard_map/all_to_all | solution.py:95
  118.3 53.0 %all-to-all-start.2 = ((bf16[2,512,16,128]{3,1,0,2:T(8,128)(2,1)}), bf16[2,512,16,128]{3,1,0,2:T(8,128)(2,1)}, u32[]{:S(2)}, u32[]{:S(2)}) async-start(bf16[2,512,16,128]{3,1,0,2:T(8,128)(2,1)} %copy.94), calls=%async_computation.2 | async-start | bytes 8388608 | tf_op jit(solution)/shard_map/all_to_all | solution.py:101
  171.3 53.1 %all-to-all-start.3 = ((bf16[2,512,16,128]{1,3,0,2:T(8,128)(2,1)}), bf16[2,512,16,128]{1,3,0,2:T(8,128)(2,1)}, u32[]{:S(2)}, u32[]{:S(2)}) async-start(bf16[2,512,16,128]{1,3,0,2:T(8,128)(2,1)} %copy.98), calls=%async_computation.3 | async-start | bytes 8388608 | tf_op jit(solution)/shard_map/all_to_all | solution.py:98
  181.1 51.2 %collective-permute-start = (bf16[2,32,32,4,128]{4,2,1,3,0:T(8,128)(2,1)}, bf16[2,32,32,4,128]{4,2,1,3,0:T(8,128)(2,1)}, u32[]{:S(2)}, u32[]{:S(2)}) collective-permute-start(bf16[2,32,32,4,128]{4,2,1,3,0:T(8,128)(2,1)} %get-tuple-element.115), channel_id=1, source_target_pairs={{4,0},{8,4},{12,8},{16,12},{20,16},{24,20},{28,24},{0,28},{5,1},{9... | collective-permute-start | bytes 6291464 | tf_op jit(solution)/shard_map/ppermute | solution.py:15
  251.4 20.6 %copy-start = (s32[4]{0:T(128)}, s32[4]{0:T(128)S(1)}, u32[]{:S(2)}) copy-start(s32[4]{0:T(128)S(1)} %get-tuple-element.203) | copy-start | bytes 52 | tf_op jit(solution)/shard_map/while
  381.7 17.1 %copy-start.1 = (s32[4]{0:T(128)S(1)}, s32[4]{0:T(128)}, u32[]{:S(2)}) copy-start(s32[4]{0:T(128)} %copy-done) | copy-start | bytes 52 | tf_op jit(solution)/shard_map/while
  398.8 20.6 %copy-start = (s32[4]{0:T(128)}, s32[4]{0:T(128)S(1)}, u32[]{:S(2)}) copy-start(s32[4]{0:T(128)S(1)} %get-tuple-element.203) | copy-start | bytes 52 | tf_op jit(solution)/shard_map/while
  531.5 18.3 %copy-start.1 = (s32[4]{0:T(128)S(1)}, s32[4]{0:T(128)}, u32[]{:S(2)}) copy-start(s32[4]{0:T(128)} %copy-done) | copy-start | bytes 52 | tf_op jit(solution)/shard_map/while
  549.8 20.6 %copy-start = (s32[4]{0:T(128)}, s32[4]{0:T(128)S(1)}, u32[]{:S(2)}) copy-start(s32[4]{0:T(128)S(1)} %get-tuple-element.203) | copy-start | bytes 52 | tf_op jit(solution)/shard_map/while
  682.5 18.3 %copy-start.1 = (s32[4]{0:T(128)S(1)}, s32[4]{0:T(128)}, u32[]{:S(2)}) copy-start(s32[4]{0:T(128)} %copy-done) | copy-start | bytes 52 | tf_op jit(solution)/shard_map/while
  700.8 20.6 %copy-start = (s32[4]{0:T(128)}, s32[4]{0:T(128)S(1)}, u32[]{:S(2)}) copy-start(s32[4]{0:T(128)S(1)} %get-tuple-element.203) | copy-start | bytes 52 | tf_op jit(solution)/shard_map/while
  833.5 18.3 %copy-start.1 = (s32[4]{0:T(128)S(1)}, s32[4]{0:T(128)}, u32[]{:S(2)}) copy-start(s32[4]{0:T(128)} %copy-done) | copy-start | bytes 52 | tf_op jit(solution)/shard_map/while
  877.6 140.5 %collective-permute-start.1 = (bf16[3,2,32,32,4,128]{5,3,2,4,1,0:T(8,128)(2,1)S(1)}, bf16[3,2,32,32,4,128]{5,3,2,4,1,0:T(8,128)(2,1)S(1)}, u32[]{:S(2)}, u32[]{:S(2)}) collective-permute-start(bf16[3,2,32,32,4,128]{5,3,2,4,1,0:T(8,128)(2,1)S(1)} %fusion.72), channel_id=1, source_target_pairs={{28,0},{0,4},{4,8},{8,12},{12,16},{16,20},{20,24},{24,28},{29,1},{... | collective-permute-start | bytes 18874376 | tf_op jit(solution)/shard_map/ppermute | solution.py:15
